TPU v7x, 32 devices: a whole 2x2x4 slice. The times are simulated.
32 devices in a mesh: row: 4 (over z), col: 8 (over y, x, core).
Axes of the slice: x: 2, y: 2, z: 4, core: 2. Of those that a mesh axis runs over, the one named last changes fastest.
Arguments:
- trace: float32 [16, 4, 8, 8, 128, 128], P(None, 'row', None, 'col'), may hold values from -6 to 6
- fill: int32 [16, 4, 8, 8], P(None, 'row', None, 'col'), may hold values 0 or 1
- pivots: float32 [2, 128, 128], replicated, may hold values from -0.046875 to 0.046875
- direct_rhs: float32 [16, 4, 16, 128], P(None, 'row'), may hold values from -6 to 6
- adjoint_rhs: float32 [16, 4, 16, 128], P(None, 'row'), may hold values from -6 to 6
Outputs:
- factored: float32 [16, 4, 8, 8, 128, 128], P(None, 'row', None, 'col')
- direct: float32 [16, 4, 16, 128], P(None, 'row')
- adjoint: float32 [16, 4, 16, 128], P(None, 'row')
- image: float32 [16, 4, 16, 128], P(None, 'row', 'col')
- back_image: float32 [8, 8, 16, 128], P(None, 'col', 'row')
All inputs are finite; a program needn't handle non-finite values. No bound on the sum of `fill` on one device may be relied on, other than what follows from the above.
Results may differ from a plain program's by a relative error of at most 0.0003.
Values sent between devices are 32-bit elements; how exact they have to be, the bound alone decides.
A program may use at most 128 MiB of HBM per device.

v0:
```python
import jax
import jax.numpy as jnp
from jax import lax
from jax.sharding import PartitionSpec as P


def from_root(x, axis, root):
    mine = lax.axis_index(axis) == root
    return lax.psum(jnp.where(mine, x, jnp.zeros_like(x)), axis)


def apply_panel(blocks, lower, upper, panel, below, global_cols):
    highest = lax.Precision.HIGHEST
    change = jnp.einsum("iab,jbc->ijac", lower, upper, precision=highest)
    keep = below[:, None] & (global_cols > panel)[None, :]
    blocks = blocks - jnp.where(keep[:, :, None, None], change, 0.0)
    target = (global_cols == panel)[None, :, None, None]
    return jnp.where(target, lower[:, None], blocks)


def shards(trace, fill, pivots, direct_rhs, adjoint_rhs):
    highest = lax.Precision.HIGHEST
    row_count = lax.axis_size("row")
    col_count = lax.axis_size("col")
    row_index = lax.axis_index("row")
    col_index = lax.axis_index("col")
    local_rows = trace.shape[0]
    local_cols = trace.shape[2]
    width = trace.shape[4]
    global_rows = jnp.arange(local_rows) * row_count + row_index
    global_cols = jnp.arange(local_cols) * col_count + col_index
    blocks = (trace * fill[:, :, :, :, None, None].astype(jnp.float32))[:, 0, :, 0]
    lowers = []
    for panel in range(2):
        below = global_rows > panel
        upper = from_root(blocks[panel // row_count], "row", panel % row_count)
        column = blocks[:, panel // col_count]
        formed = jnp.einsum("iab,bc->iac", column, pivots[panel], precision=highest)
        lower = from_root(jnp.where(below[:, None, None], formed, column), "col", panel % col_count)
        blocks = apply_panel(blocks, lower, upper, panel, below, global_cols)
        lowers.append(jnp.where(below[:, None, None], lower, 0.0))
    solution = direct_rhs[:, 0]
    for panel in range(2):
        pivot_part = from_root(solution[panel // row_count], "row", panel % row_count)
        solution = solution - jnp.einsum(
            "iab,mb->ima", lowers[panel], pivot_part, precision=highest
        )
    adjoint = adjoint_rhs[:, 0]
    for panel in (1, 0):
        partial_sum = jnp.einsum("iab,ima->mb", lowers[panel], adjoint, precision=highest)
        total = lax.psum(partial_sum, "row")
        owner = row_index == panel % row_count
        adjoint = adjoint.at[panel // row_count].add(jnp.where(owner, -total, 0.0))
    scale = (local_rows * row_count * width) ** (-0.5)
    modes = solution.shape[1]
    gathered = lax.all_gather(solution[:, None], "row", axis=1, tiled=True)
    by_column = gathered.reshape(local_cols, col_count, modes, width)
    mine = lax.dynamic_index_in_dim(by_column, col_index, 1, keepdims=False)
    image_terms = jnp.einsum("ijab,jmb->ima", blocks, mine, precision=highest) * scale
    image = lax.psum_scatter(image_terms, "col", scatter_dimension=1, tiled=True)
    back_terms = jnp.einsum("ijab,ima->jmb", blocks, adjoint, precision=highest) * scale
    back = lax.psum_scatter(back_terms, "row", scatter_dimension=1, tiled=True)
    return (
        blocks[:, None, :, None],
        solution[:, None],
        adjoint[:, None],
        image[:, None],
        back[:, None],
    )


def solution(mesh):
    placed = (
        P(None, "row", None, "col", None, None),
        P(None, "row", None, "col"),
        P(),
        P(None, "row", None, None),
        P(None, "row", None, None),
    )
    return jax.shard_map(
        shards,
        mesh=mesh,
        in_specs=placed,
        out_specs=(
            P(None, "row", None, "col", None, None),
            P(None, "row", None, None),
            P(None, "row", None, None),
            P(None, "row", "col", None),
            P(None, "col", "row", None),
        ),
        check_vma=False,
    )
```

profile of v0, /device:TPU:0, one launch (start us, length us, event | category | flops | bytes accessed | tf_op | source)
XLA Modules:
  0.0 313.8 jit_solution(13680377646594469356)
XLA Ops:
  7.2 0.7 convert_bitcast_fusion
  7.9 4.0 %fusion.51 = f32[16,8,128,128]{3,2,0,1:T(8,128)S(1)} fusion(f32[16,8]{0,1:T(8,128)S(1)} %convert_bitcast_fusion, f32[16,1,8,1,128,128]{5,4,3,2,1,0:T(8,128)} %param.9), kind=kLoop, calls=%fused_computation.77 | loop fusion | flops 2097152 | bytes 16777728 | tf_op jit(solution)/shard_map/squeeze | solution.py:32
  12.0 2.0 fusion.4
  14.1 7.4 %copy_multiply_fusion = f32[16,1,8,1,128,128]{5,4,0,2,3,1:T(8,128)} fusion(f32[16,1,8,1,128,128]{5,4,3,2,1,0:T(8,128)} %param.9, f32[16,8]{0,1:T(8,128)S(1)} %convert_bitcast_fusion), kind=kLoop, calls=%fused_computation.6 | loop fusion | flops 2097152 | bytes 16777728 | tf_op jit(solution)/shard_map/mul | solution.py:32
  21.5 2.0 fusion.19
  23.6 0.1 broadcast_and_fusion.1
  23.7 0.1 broadcast_and_fusion
  23.7 49.9 %all-reduce.7.cloned.1.call-done = f32[16,128,128]{2,1,0:T(8,128)} async-done(((f32[16,128,128]{2,1,0:T(8,128)}), f32[16,128,128]{2,1,0:T(8,128)}) %all-reduce.7.cloned.1.call-update) | async-done | bytes 1048592 | tf_op jit(solution)/shard_map/psum | solution.py:9
  73.6 40.3 %all-reduce.9.cloned.1.call-done = f32[8,128,128]{2,1,0:T(8,128)} async-done(((f32[8,128,128]{2,1,0:T(8,128)}), f32[8,128,128]{2,1,0:T(8,128)}) %all-reduce.9.cloned.1.call-update) | async-done | bytes 524304 | tf_op jit(solution)/shard_map/psum | solution.py:9
  113.9 10.3 %fusion.3 = f32[16,8,128,128]{3,2,0,1:T(8,128)S(1)} fusion(f32[16,128,128]{2,1,0:T(8,128)} %all-reduce.7.cloned.1.call-done, pred[8]{0:T(512)(128)(4,1)S(1)} %get-tuple-element.44, pred[16,8]{0,1:T(8,128)(4,1)S(1)} %broadcast_and_fusion.1, f32[8,128,128]{2,1,0:T(8,128)} %all-reduce.9.cloned.1.call-done, f32[16,1,8,1,128,128]{5,4,0,2,3,1:T(8,128)} %copy_multiply_fusion), kind=kOutput, calls=%fused_computation.5 | convolution fusion | flops 3227516928 | bytes 18350216 | tf_op jit(solution)/shard_map/iab,jbc->ijac/dot_general | solution.py:14
  124.2 3.4 %copy-done.1 = f32[16,8,128,128]{3,2,0,1:T(8,128)} copy-done((f32[16,8,128,128]{3,2,0,1:T(8,128)}, f32[16,8,128,128]{3,2,0,1:T(8,128)S(1)}, u32[]{:S(2)}) %copy-start.1) | copy-done | bytes 8388632
  127.6 2.0 fusion.5
  129.8 1.9 fusion.18
  131.7 54.6 %all-reduce.11.cloned.1.call-done = f32[16,128,128]{2,1,0:T(8,128)} async-done(((f32[16,128,128]{2,1,0:T(8,128)}), f32[16,128,128]{2,1,0:T(8,128)}) %all-reduce.11.cloned.1.call-update) | async-done | bytes 1048592 | tf_op jit(solution)/shard_map/psum | solution.py:9
  186.3 2.0 convolution_bitcast_fusion.5
  188.3 19.1 %all-reduce.1 = (f32[16,128]{1,0:T(8,128)S(1)}, f32[16,128]{1,0:T(8,128)S(1)}) all-reduce(f32[16,128]{1,0:T(8,128)S(1)} %select_bitcast_fusion, f32[16,128]{1,0:T(8,128)S(1)} %convolution_bitcast_fusion.5), channel_id=1, replica_groups=mesh['row'=4,'col'=8] {'row'}, use_global_device_ids=true, to_apply=%region_4.5 | all-reduce | flops 4096 | bytes 32768 | tf_op jit(solution)/shard_map/psum | solution.py:9
  207.4 1.0 fusion.6
  208.4 0.7 convolution_bitcast_fusion.4
  209.1 15.8 %all-reduce = (f32[16,128]{1,0:T(8,128)S(1)}, f32[16,128]{1,0:T(8,128)S(1)}) all-reduce(f32[16,128]{1,0:T(8,128)S(1)} %fusion.37, f32[16,128]{1,0:T(8,128)S(1)} %convolution_bitcast_fusion.4), channel_id=1, replica_groups=mesh['row'=4,'col'=8] {'row'}, use_global_device_ids=true, to_apply=%region_5.6 | all-reduce | flops 4096 | bytes 32768 | tf_op jit(solution)/shard_map/psum | solution.py:9
  225.0 1.3 all-reduce.13.cloned.1.call-done
  226.3 10.2 %fusion.1 = f32[16,8,128,128]{3,2,0,1:T(8,128)S(1)} fusion(f32[16,8,128,128]{3,2,0,1:T(8,128)} %copy-done.1, f32[16,128,128]{2,1,0:T(8,128)} %all-reduce.11.cloned.1.call-done, pred[8]{0:T(512)(128)(4,1)S(1)} %broadcast_compare_fusion.3, pred[16,8]{0,1:T(8,128)(4,1)S(1)} %broadcast_and_fusion, f32[8,128,128]{2,1,0:T(8,128)} %all-reduce.13.cloned.1.call-done), kind=kOutput, calls=%fused_computation.2 | convolution fusion | flops 3227516928 | bytes 18350216 | tf_op jit(solution)/shard_map/iab,jbc->ijac/dot_general | solution.py:14
  236.5 3.2 %copy-done = f32[16,8,128,128]{3,2,0,1:T(8,128)} copy-done((f32[16,8,128,128]{3,2,0,1:T(8,128)}, f32[16,8,128,128]{3,2,0,1:T(8,128)S(1)}, u32[]{:S(2)}) %copy-start) | copy-done | bytes 8388632
  239.7 4.1 %fusion.11 = f32[8,16,128]{2,1,0:T(8,128)S(1)} fusion(f32[16,8,128,128]{3,2,0,1:T(8,128)S(1)} %fusion.1, f32[16,16,128]{2,1,0:T(8,128)S(1)} %bitcast_dynamic-update-slice_fusion), kind=kOutput, calls=%fused_computation.20 | convolution fusion | flops 402669568 | bytes 8585216 | tf_op jit(solution)/shard_map/ijab,ima->jmb/dot_general | solution.py:61
  243.8 0.7 copy.29
  244.5 1.0 fusion.7
  245.6 16.2 %all-gather = f32[16,64,128]{2,1,0:T(8,128)S(1)} all-gather(f32[16,16,128]{2,1,0:T(8,128)S(1)} %fusion.7), channel_id=2, replica_groups=mesh['row'=4,'col'=8] {'row'}, dimensions={1}, use_global_device_ids=true | all-gather | bytes 655360 | tf_op jit(solution)/shard_map/all_gather | solution.py:56
  261.8 9.2 %fusion.9 = f32[16,16,128]{2,1,0:T(8,128)S(1)} fusion(f32[16,8,128,128]{3,2,0,1:T(8,128)} %copy-done, f32[8,8,16,128]{3,2,1,0:T(8,128)S(1)} %bitcast.139, s32[]{:T(128)S(6)} %select_n.128), kind=kOutput, calls=%fused_computation.17 | convolution fusion | flops 402685952 | bytes 8585220 | tf_op jit(solution)/shard_map/ijab,jmb->ima/dot_general | solution.py:59
  271.0 0.7 copy.28
  271.7 7.9 %copy.30 = f32[16,1,8,1,128,128]{5,4,3,2,1,0:T(8,128)} copy(f32[16,1,8,1,128,128]{5,4,0,2,3,1:T(8,128)} %bitcast.137) | data formatting | bytes 16777216
  279.6 1.3 copy.33
  281.0 24.6 %reduce-scatter.3.cloned.1.call-done = f32[16,2,128]{2,0,1:T(8,128)} async-done(((f32[16,16,128]{2,0,1:T(8,128)}), f32[16,2,128]{2,0,1:T(8,128)}) %reduce-scatter.3.cloned.1.call-update) | async-done | bytes 16400 | tf_op jit(solution)/shard_map/reduce_scatter | solution.py:60
  305.6 1.3 copy.32
  (39 shorter events, 0.5 us)
Async XLA Ops:
  7.2 66.4 %all-reduce.7.cloned.1.call-start = ((), (), s32[]{:S(2)}) async-start(), calls=%async_computation.2 | async-start | bytes 2097152 | tf_op jit(solution)/shard_map/psum | solution.py:9
  7.9 4.0 %copy-start.8 = (f32[2,128,128]{2,1,0:T(8,128)S(1)}, f32[2,128,128]{2,1,0:T(8,128)}, u32[]{:S(2)}) copy-start(f32[2,128,128]{2,1,0:T(8,128)} %param.11) | copy-start | bytes 393220
  14.0 99.9 %all-reduce.9.cloned.1.call-start = ((), (), s32[]{:S(2)}) async-start(), calls=%async_computation.3 | async-start | bytes 1048576 | tf_op jit(solution)/shard_map/psum | solution.py:9
  23.5 162.8 %all-reduce.11.cloned.1.call-start = ((), (), s32[]{:S(2)}) async-start(), calls=%async_computation.4 | async-start | bytes 2097152 | tf_op jit(solution)/shard_map/psum | solution.py:9
  113.9 15.8 %copy-start.5 = (f32[16,1,16,128]{3,2,1,0:T(8,128)S(1)}, f32[16,1,16,128]{3,2,1,0:T(8,128)}, u32[]{:S(2)}) copy-start(f32[16,1,16,128]{3,2,1,0:T(8,128)} %param.13) | copy-start | bytes 393220
  113.9 15.9 %copy-start.7 = (f32[16,1,16,128]{3,2,1,0:T(8,128)S(1)}, f32[16,1,16,128]{3,2,1,0:T(8,128)}, u32[]{:S(2)}) copy-start(f32[16,1,16,128]{3,2,1,0:T(8,128)} %param.12) | copy-start | bytes 393220
  113.9 93.5 %copy-start.2 = (f32[16,128,128]{2,1,0:T(8,128)S(1)}, f32[16,128,128]{2,1,0:T(8,128)}, u32[]{:S(2)}) copy-start(f32[16,128,128]{2,1,0:T(8,128)} %all-reduce.7.cloned.1.call-done) | copy-start | bytes 3145732
  124.2 3.4 %copy-start.1 = (f32[16,8,128,128]{3,2,0,1:T(8,128)}, f32[16,8,128,128]{3,2,0,1:T(8,128)S(1)}, u32[]{:S(2)}) copy-start(f32[16,8,128,128]{3,2,0,1:T(8,128)S(1)} %fusion.3) | copy-start | bytes 25165828
  129.6 96.7 %all-reduce.13.cloned.1.call-start = ((), (), s32[]{:S(2)}) async-start(), calls=%async_computation.5 | async-start | bytes 1048576 | tf_op jit(solution)/shard_map/psum | solution.py:9
  131.7 147.9 %reduce-scatter.5.cloned.1.call-start = ((), (), s32[]{:S(2)}) async-start(), calls=%async_computation.7 | async-start | bytes 81920 | tf_op jit(solution)/shard_map/reduce_scatter | solution.py:62
  224.9 11.6 %copy-start.4 = (f32[16,16,128]{2,1,0:T(8,128)}, f32[16,16,128]{2,1,0:T(8,128)S(1)}, u32[]{:S(2)}) copy-start(f32[16,16,128]{2,1,0:T(8,128)S(1)} %bitcast_dynamic-update-slice_fusion) | copy-start | bytes 393220
  236.5 3.2 %copy-start = (f32[16,8,128,128]{3,2,0,1:T(8,128)}, f32[16,8,128,128]{3,2,0,1:T(8,128)S(1)}, u32[]{:S(2)}) copy-start(f32[16,8,128,128]{3,2,0,1:T(8,128)S(1)} %fusion.1) | copy-start | bytes 25165828
  239.7 4.8 %copy-start.3 = (f32[16,128,128]{2,1,0:T(8,128)S(1)}, f32[16,128,128]{2,1,0:T(8,128)}, u32[]{:S(2)}) copy-start(f32[16,128,128]{2,1,0:T(8,128)} %all-reduce.11.cloned.1.call-done) | copy-start | bytes 3145732
  244.5 61.1 %reduce-scatter.3.cloned.1.call-start = ((), (), s32[]{:S(2)}) async-start(), calls=%async_computation.6 | async-start | bytes 147456 | tf_op jit(solution)/shard_map/reduce_scatter | solution.py:60
  245.6 34.1 %copy-start.6 = (f32[16,16,128]{2,1,0:T(8,128)}, f32[16,16,128]{2,1,0:T(8,128)S(1)}, u32[]{:S(2)}) copy-start(f32[16,16,128]{2,1,0:T(8,128)S(1)} %fusion.7) | copy-start | bytes 393220
Sparse Core Ops, SparseCore 0:
  14.1 59.4 all-reduce.6
  75.9 37.8 all-reduce.8
  129.8 56.5 all-reduce.10
  188.5 37.7 all-reduce.12
  244.6 19.0 reduce-scatter.4
  271.9 33.6 reduce-scatter.2
where the time goes:
time: 314 us
  waiting for transfers between devices  171 us (54%)
  blocking collectives  51.1 us (16%)
  matrix products  42.5 us (14%)
  local copies, waits for them, and re-layouts  18.6 us (6%)
  other arithmetic  16.2 us (5%)
  between operations  14.3 us (5%)
    psum x4, waiting for transfers between devices, from_root(): return lax.psum(jnp.where(mine, x, jnp.zeros_like(x)), axis)  146 us
    psum x2, blocking collectives, from_root(): return lax.psum(jnp.where(mine, x, jnp.zeros_like(x)), axis)  34.9 us
    reduce_scatter x1, waiting for transfers between devices, shards(): lax.psum_scatter(image_terms, 'col', scatter_dimension=1, tiled=True)  24.6 us
    dot_general x2, matrix products, apply_panel(): change = jnp.einsum('iab,jbc->ijac', lower, upper, precision=highest)  20.5 us
    unnamed x22, local copies, waits for them, and re-layouts  17.2 us
    all_gather x1, blocking collectives, shards(): gathered = lax.all_gather(solution[:, None], 'row', axis=1, tiled=True)  16.2 us
    dot_general x1, matrix products, shards(): jnp.einsum('ijab,jmb->ima', blocks, mine, precision=highest) * scale  9.2 us
    mul x1, other arithmetic, shards(): trace * fill[:, :, :, :, None, None].astype(jnp.float32)  7.39 us
  transfers between devices with their start and end apart: 6, of which 5 were waited for; matrix products, arithmetic and copies ran while one was open for 11% of the time, Pallas kernels for 0%

commit v1 on v0

v1 whole, which is shorter than its diff:
```python
import functools

import jax
import jax.numpy as jnp
from jax import lax
from jax.experimental import pallas as pl
from jax.experimental.pallas import tpu as pltpu
from jax.sharding import PartitionSpec as P

F32 = jnp.float32
BF16 = jnp.bfloat16
NN = (((1,), (0,)), ((), ()))
NT = (((1,), (1,)), ((), ()))


def split(x):
    high = x.astype(BF16)
    return high, (x - high.astype(F32)).astype(BF16)


def mul(a, b, dims):
    return lax.dot_general(a, b, dims, preferred_element_type=F32)


def dot3(a, b, dims):
    ah, al = split(a)
    bh, bl = split(b)
    return mul(ah, bh, dims) + mul(ah, bl, dims) + mul(al, bh, dims)


def stack(x):
    high, low = split(x)
    return jnp.concatenate([high, low], axis=0)


def thin(pair, bh, bl, dims):
    half = pair.shape[0] // 2
    both = mul(pair, bh, dims)
    return both[:half] + both[half:] + mul(pair[:half], bl, dims)


def comm_kernel(
    n_row, n_col, fill, piv, direct_rhs, adjoint_rhs, trace,
    fcol, upper, y_out, z_out, image, back,
    colbuf, rowbuf, mbuf, small, wloc, wrecv, ysel, ypair, zpair,
    img_p, img_t, img_r, back_p, back_t, back_r,
    load_sem, m_sem, sm_send, sm_recv, ring_send, ring_recv, sib_send, sib_recv,
    row_up, row_down, row_recv, w_send, w_recv, y_send, y_recv,
    is_send, is_recv, bs_send, bs_recv,
):
    rows, cols = mbuf.shape[0], mbuf.shape[1]
    modes = y_out.shape[1]
    width = y_out.shape[2]
    img_modes, back_modes = modes // n_col, modes // n_row
    scale = (rows * n_row * width) ** (-0.5)
    p = lax.axis_index("row")
    q = lax.axis_index("col")
    chips = n_col // 2
    deep = chips // 2
    chip, core = q // 2, q % 2
    cy, cx = chip // 2, chip % 2
    pos = cx * (cy + 1) + (1 - cx) * ((chips - cy) % chips)

    def at_pos(r):
        side = 1 - ((r + chips - 1) % chips) // deep
        return (side * ((r - 1) * 2 + 1) + (1 - side) * (((chips - r) % chips) * 2)) * 2 + core

    after = at_pos((pos + 1) % chips)
    before = at_pos((pos + chips - 1) % chips)
    sibling = chip * 2 + 1 - core
    half = rows // 2

    def to(src, dst, send, recv, row, col):
        return pltpu.make_async_remote_copy(
            src_ref=src, dst_ref=dst, send_sem=send, recv_sem=recv,
            device_id=(row, col), device_id_type=pl.DeviceIdType.MESH,
        )

    col_load = pltpu.make_async_copy(trace.at[:, 0], colbuf.at[core, pl.ds(0, rows)], load_sem.at[0])
    row_load = pltpu.make_async_copy(trace.at[0], rowbuf.at[lax.rem(p, 2)], load_sem.at[1])

    @pl.when(q < 2)
    def _():
        col_load.start()

    @pl.when(p < 2)
    def _():
        row_load.start()

    m_load = pltpu.make_async_copy(trace, mbuf, m_sem)
    m_load.start()

    barrier = pltpu.get_barrier_semaphore()
    for d in range(1, n_col):
        pl.semaphore_signal(barrier, inc=1, device_id=(p, (q + d) % n_col), device_id_type=pl.DeviceIdType.MESH)
    for d in range(1, n_row):
        pl.semaphore_signal(barrier, inc=1, device_id=((p + d) % n_row, q), device_id_type=pl.DeviceIdType.MESH)

    @pl.when(q < 2)
    def _():
        col_load.wait()

        def mask(a, _):
            colbuf[core, a] = colbuf[core, a] * fill[a, 0].astype(F32)
            return 0

        lax.fori_loop(0, rows, mask, 0)

    @pl.when(p < 2)
    def _():
        row_load.wait()
        slot = lax.rem(p, 2)

        def mask(c, _):
            rowbuf[slot, c] = rowbuf[slot, c] * fill[0, c].astype(F32)
            return 0

        lax.fori_loop(0, cols, mask, 0)
        small[slot, 0] = direct_rhs[0]
        small[slot, 1] = adjoint_rhs[0]

    pl.semaphore_wait(barrier, n_col + n_row - 2)

    def small_copy(kind, d):
        src = (direct_rhs, adjoint_rhs)[kind].at[0]
        return to(src, small.at[lax.rem(p, 2), kind], sm_send.at[kind, d], sm_recv.at[lax.rem(p, 2), kind], (p + d) % n_row, q)

    def ring(block, dest):
        ref = colbuf.at[core, block]
        return to(ref, ref, ring_send.at[block], ring_recv.at[block], p, dest)

    def sib(block, which):
        ref = colbuf.at[which, block]
        return to(ref, ref, sib_send.at[block], sib_recv.at[block], p, sibling)

    def row_copy(k, c, upward):
        ref = rowbuf.at[k, c]
        sems = row_up if upward else row_down
        dest = lax.rem(p + (1 if upward else n_row - 1), n_row)
        return to(ref, ref, sems.at[k, c], row_recv.at[k, c], dest, q)

    @pl.when(pos == 0)
    def _():
        def send(s, _):
            ring(s, after).start()
            ring(half + s, before).start()
            return 0

        lax.fori_loop(0, half, send, 0)

    for k in range(2):
        @pl.when(p == k)
        def _(k=k):
            def send(c, _):
                if k + 1 < n_row:
                    row_copy(k, c, True).start()
                if k > 0:
                    row_copy(k, c, False).start()
                return 0

            lax.fori_loop(0, cols, send, 0)

    @pl.when(p < 2)
    def _():
        for d in range(1, n_row):
            for kind in range(2):
                small_copy(kind, d).start()

    @pl.when(pos == 0)
    def _():
        def send(s, _):
            sib(s, core).start()
            return 0

        lax.fori_loop(0, rows, send, 0)

    def ring_step(block, forward):
        @pl.when(pos != 0)
        def _():
            dest = after if forward else before
            ring(block, dest).wait_recv()
            stop = chips - 1 if forward else 1

            @pl.when(pos != stop)
            def _():
                ring(block, dest).start()

            sib(block, core).start()

    def row_step(c):
        for k in range(2):
            @pl.when(p != k)
            def _(k=k):
                row_copy(k, c, True).wait_recv()

                @pl.when((p > k) & (p + 1 < n_row))
                def _():
                    row_copy(k, c, True).start()

                if k > 1:
                    @pl.when((p < k) & (p > 0))
                    def _():
                        row_copy(k, c, False).start()

    def ring_pair(s, _):
        ring_step(s, True)
        ring_step(half + s, False)
        return 0

    lax.fori_loop(0, half // 2, ring_pair, 0)
    row_step(0)

    @pl.when(pos == 0)
    def _():
        colbuf[core, rows] = rowbuf[1 - core, 0]
        lax.fori_loop(half // 2, half - 2, ring_pair, 0)

    @pl.when(pos != 0)
    def _():
        lax.fori_loop(half // 2, half - 2, ring_pair, 0)

    row_step(1)

    @pl.when(pos == 0)
    def _():
        ring(rows, after).start()
        sib(rows, core).start()

    lax.fori_loop(half - 2, half, ring_pair, 0)
    row_step(2)
    ring_step(rows, True)

    def sib_wait(block, _):
        sib(block, 1 - core).wait_recv()
        return 0

    lax.fori_loop(0, rows + 1, sib_wait, 0)
    for k in range(2):
        @pl.when(p != k)
        def _(k=k):
            for kind in range(2):
                to(small.at[k, kind], small.at[k, kind], sm_send.at[kind, 0], sm_recv.at[k, kind], p, sibling).wait_recv()
    row_step(3)

    p0h, p0l = split(piv[0])
    p1h, p1l = split(piv[1])
    u01h, u01l = split(colbuf[1, rows])
    c10h, c10l = split(colbuf[0, rows])
    l10 = mul(c10h, p0h, NN) + mul(c10h, p0l, NN) + mul(c10l, p0h, NN)
    l10h, l10l = split(l10)
    y0 = stack(small[0, 0])
    y1 = stack(small[1, 0] - thin(y0, l10h, l10l, NT))
    wloc[...] = jnp.zeros_like(wloc)

    def form(a, _):
        index = a * n_row + p
        raw0, raw1 = colbuf[0, a], colbuf[1, a]
        l0 = jnp.where(index > 0, 1.0, 0.0) * dot3_split(raw0, p0h, p0l)
        l0h, l0l = split(l0)
        mid = raw1 - (mul(l0h, u01h, NN) + mul(l0h, u01l, NN) + mul(l0l, u01h, NN))
        below = jnp.where(index > 1, 1.0, 0.0)
        l1 = below * dot3_split(mid, p1h, p1l)
        l1h, l1l = split(l1)
        fcol[0, a] = jnp.where(index > 0, l0, raw0)
        fcol[1, a] = jnp.where(index > 1, l1, mid)
        y_out[a] = direct_rhs[a] - thin(y0, l0h, l0l, NT) - thin(y1, l1h, l1l, NT)
        za = stack(adjoint_rhs[a])
        wloc[0] += below * thin(za, l0h, l0l, NN)
        wloc[1] += below * thin(za, l1h, l1l, NN)
        return 0

    quarter = rows // 4
    for g in range(4):
        lax.fori_loop(g * quarter, (g + 1) * quarter, form, 0)
        if g < 3:
            row_step(4 + g)

    owner = q % n_row
    step = n_col // n_row
    for c in range(cols):
        @pl.when(p == owner)
        def _(c=c):
            ysel[c] = y_out[c * step + q // n_row]

    def w_copy(d):
        return to(wloc, wrecv.at[p], w_send.at[d], w_recv.at[p], (p + d) % n_row, q)

    def y_copy(d):
        return to(ysel, ysel, y_send.at[d], y_recv, (p + d) % n_row, q)

    for d in range(1, n_row):
        w_copy(d).start()

    @pl.when(p == owner)
    def _():
        for d in range(1, n_row):
            y_copy(d).start()

    for c in range(7, cols):
        row_step(c)

    def form_upper(c, _):
        u0 = rowbuf[0, c]
        u0h, u0l = split(u0)
        upper[0, c] = u0
        upper[1, c] = rowbuf[1, c] - (mul(l10h, u0h, NN) + mul(l10h, u0l, NN) + mul(l10l, u0h, NN))
        return 0

    lax.fori_loop(0, cols, form_upper, 0)

    w0, w1 = wloc[0], wloc[1]
    for d in range(1, n_row):
        peer = (p + d) % n_row
        to(wloc, wrecv.at[peer], w_send.at[d], w_recv.at[peer], peer, q).wait_recv()
        w0 = w0 + wrecv[peer, 0]
        w1 = w1 + wrecv[peer, 1]
    z1 = small[1, 1] - w1
    z1l = thin(stack(z1), l10h, l10l, NN)
    z0 = small[0, 1] - w0 - z1l
    z_out[...] = adjoint_rhs[...]
    z_out[0] = jnp.where(p == 0, z0, jnp.where(p == 1, z1, adjoint_rhs[0]))

    @pl.when(p != owner)
    def _():
        to(ysel, ysel, y_send.at[0], y_recv, p, sibling).wait_recv()

    m_load.wait()

    wz0 = stack(wloc[0] + jnp.where(p == 1, 1.0, 0.0) * z1l)
    wz1 = stack(wloc[1])
    v0 = jnp.zeros((modes, width), F32)
    v1 = jnp.zeros((modes, width), F32)
    for c in range(cols):
        inner = jnp.where(q > 1, 1.0, 0.0) if c == 0 else 1.0
        yc = stack(ysel[c])
        ypair[c] = yc
        u0h, u0l = split(upper[0, c] * inner)
        u1h, u1l = split(upper[1, c] * inner)
        v0 = v0 + thin(yc, u0h, u0l, NT)
        v1 = v1 + thin(yc, u1h, u1l, NT)
        back_p[c] = -(thin(wz0, u0h, u0l, NN) + thin(wz1, u1h, u1l, NN))
    v0 = stack(v0)
    v1 = stack(v1)

    def products(a, _):
        index = a * n_row + p
        za = stack(z_out[a])
        l0h, l0l = split(fcol[0, a] * jnp.where(index > 0, 1.0, 0.0))
        l1h, l1l = split(fcol[1, a] * jnp.where(index > 1, 1.0, 0.0))
        acc = -(thin(v0, l0h, l0l, NT) + thin(v1, l1h, l1l, NT))
        for c in range(cols):
            m = mbuf[a, c] * fill[a, c].astype(F32)
            if c == 0:
                m = jnp.where(q == 0, fcol[0, a], jnp.where(q == 1, fcol[1, a], m))
            mh, ml = split(m)
            acc = acc + thin(ypair[c], mh, ml, NT)
            back_p[c] += thin(za, mh, ml, NN)
        img_p[a] = acc
        return 0

    lax.fori_loop(0, rows, products, 0)
    for m in range(modes):
        img_t[m] = img_p[:, m, :] * scale
        back_t[m] = back_p[:, m, :] * scale

    def img_copy(d):
        dest = (q + d) % n_col
        return to(img_t.at[pl.ds(dest * img_modes, img_modes)], img_r.at[q], is_send.at[d], is_recv.at[q], p, dest)

    def back_copy(d):
        dest = (p + d) % n_row
        return to(back_t.at[pl.ds(dest * back_modes, back_modes)], back_r.at[p], bs_send.at[d], bs_recv.at[p], dest, q)

    for d in range(1, n_col):
        img_copy(d).start()
    for d in range(1, n_row):
        back_copy(d).start()

    total = img_t[pl.ds(q * img_modes, img_modes)]
    for d in range(1, n_col):
        peer = (q + d) % n_col
        to(img_r.at[peer], img_r.at[peer], is_send.at[d], is_recv.at[peer], p, peer).wait_recv()
        total = total + img_r[peer]
    image[...] = total
    total = back_t[pl.ds(p * back_modes, back_modes)]
    for d in range(1, n_row):
        peer = (p + d) % n_row
        to(back_r.at[peer], back_r.at[peer], bs_send.at[d], bs_recv.at[peer], peer, q).wait_recv()
        total = total + back_r[peer]
    back[...] = total

    for d in range(1, n_col):
        img_copy(d).wait_send()
    for d in range(1, n_row):
        back_copy(d).wait_send()
        w_copy(d).wait_send()

    @pl.when(p == owner)
    def _():
        for d in range(1, n_row):
            y_copy(d).wait_send()

    @pl.when(p < 2)
    def _():
        for d in range(1, n_row):
            for kind in range(2):
                small_copy(kind, d).wait_send()

    def drain_sib(block, _):
        sib(block, core).wait_send()
        return 0

    lax.fori_loop(0, rows + 1, drain_sib, 0)

    def drain(low, high, stop):
        @pl.when(pos != stop)
        def _():
            def one(block, _):
                ring(block, after).wait_send()
                return 0

            lax.fori_loop(low, high, one, 0)

    drain(0, half, chips - 1)
    drain(half, rows, 1)
    drain(rows, rows + 1, chips - 1)
    for k in range(2):
        @pl.when((p >= k) & (p + 1 < n_row))
        def _(k=k):
            def one(c, _):
                row_copy(k, c, True).wait_send()
                return 0

            lax.fori_loop(0, cols, one, 0)

    @pl.when(p == 1)
    def _():
        def one(c, _):
            row_copy(1, c, False).wait_send()
            return 0

        lax.fori_loop(0, cols, one, 0)


def dot3_split(a, bh, bl):
    ah, al = split(a)
    return mul(ah, bh, NN) + mul(ah, bl, NN) + mul(al, bh, NN)


def update_kernel(
    n_row, tile, fill, fcol, upper, y_in, z_in, img_in, back_in, trace,
    out, y_out, z_out, image, back, uh, ul,
):
    step = pl.program_id(0)
    p = lax.axis_index("row")
    q = lax.axis_index("col")
    cols, width = trace.shape[1], trace.shape[2]

    @pl.when(step == 0)
    def _():
        for k in range(2):
            for c in range(cols):
                high, low = split(upper[k, c])
                uh[k * width:(k + 1) * width, c * width:(c + 1) * width] = high
                ul[k * width:(k + 1) * width, c * width:(c + 1) * width] = low
        y_out[...] = y_in[...]
        z_out[...] = z_in[...]
        for m in range(img_in.shape[0]):
            image[:, m, :] = img_in[m]
        for m in range(back_in.shape[0]):
            back[:, m, :] = back_in[m]

    for t in range(tile):
        a = step * tile + t
        index = a * n_row + p
        l0h, l0l = split(fcol[0, t] * jnp.where(index > 0, 1.0, 0.0))
        l1h, l1l = split(fcol[1, t] * jnp.where(index > 1, 1.0, 0.0))
        lh = jnp.concatenate([l0h, l1h], axis=1)
        ll = jnp.concatenate([l0l, l1l], axis=1)
        for c in range(0, cols, 2):
            bh = uh[:, c * width:(c + 2) * width]
            bl = ul[:, c * width:(c + 2) * width]
            change = mul(lh, bh, NN) + mul(lh, bl, NN) + mul(ll, bh, NN)
            for e in range(2):
                value = trace[t, c + e] * fill[a, c + e].astype(F32) - change[:, e * width:(e + 1) * width]
                if c + e == 0:
                    value = jnp.where(q == 0, fcol[0, t], jnp.where(q == 1, fcol[1, t], value))
                out[t, c + e] = value


def shards(trace, fill, pivots, direct_rhs, adjoint_rhs):
    n_row, n_col = lax.axis_size("row"), lax.axis_size("col")
    rows, cols, width = trace.shape[0], trace.shape[2], trace.shape[4]
    modes = direct_rhs.shape[2]
    blocks = trace.reshape(rows, cols, width, width)
    flags = fill.reshape(rows, cols)
    direct_rhs, adjoint_rhs = direct_rhs[:, 0], adjoint_rhs[:, 0]
    mi, mb = modes // n_col, modes // n_row
    vmem = pl.BlockSpec(memory_space=pltpu.VMEM)
    smem = pl.BlockSpec(memory_space=pltpu.SMEM)
    shape = jax.ShapeDtypeStruct
    dma = pltpu.SemaphoreType.DMA
    fcol, upper, y, z, image, back = pl.pallas_call(
        functools.partial(comm_kernel, n_row, n_col),
        out_shape=(
            shape((2, rows, width, width), F32),
            shape((2, cols, width, width), F32),
            shape((rows, modes, width), F32),
            shape((rows, modes, width), F32),
            shape((mi, rows, width), F32),
            shape((mb, cols, width), F32),
        ),
        in_specs=[smem, vmem, vmem, vmem, pl.BlockSpec(memory_space=pl.ANY)],
        out_specs=[vmem] * 6,
        scratch_shapes=[
            pltpu.VMEM((2, rows + 1, width, width), F32),
            pltpu.VMEM((2, cols, width, width), F32),
            pltpu.VMEM((rows, cols, width, width), F32),
            pltpu.VMEM((2, 2, modes, width), F32),
            pltpu.VMEM((2, modes, width), F32),
            pltpu.VMEM((n_row, 2, modes, width), F32),
            pltpu.VMEM((cols, modes, width), F32),
            pltpu.VMEM((cols, 2 * modes, width), BF16),
            pltpu.VMEM((8, width), F32),
            pltpu.VMEM((rows, modes, width), F32),
            pltpu.VMEM((modes, rows, width), F32),
            pltpu.VMEM((n_col, mi, rows, width), F32),
            pltpu.VMEM((cols, modes, width), F32),
            pltpu.VMEM((modes, cols, width), F32),
            pltpu.VMEM((n_row, mb, cols, width), F32),
            dma((2,)), dma,
            dma((2, n_row)), dma((2, 2)),
            dma((rows + 1,)), dma((rows + 1,)), dma((rows + 1,)), dma((rows + 1,)),
            dma((2, cols)), dma((2, cols)), dma((2, cols)),
            dma((n_row,)), dma((n_row,)), dma((n_row,)), dma,
            dma((n_col,)), dma((n_col,)), dma((n_row,)), dma((n_row,)),
        ],
        compiler_params=pltpu.CompilerParams(
            collective_id=0, has_side_effects=True, vmem_limit_bytes=40 * 1024 * 1024
        ),
    )(flags, pivots, direct_rhs, adjoint_rhs, blocks)

    tile = 2
    whole = lambda x: pl.BlockSpec(x.shape, lambda i: (0,) * x.ndim)
    outs = (
        shape(blocks.shape, F32),
        shape(y.shape, F32),
        shape(z.shape, F32),
        shape((rows, mi, width), F32),
        shape((cols, mb, width), F32),
    )
    factored, direct, adjoint, image, back = pl.pallas_call(
        functools.partial(update_kernel, n_row, tile),
        out_shape=outs,
        grid=(rows // tile,),
        in_specs=[
            smem,
            pl.BlockSpec((2, tile, width, width), lambda i: (0, i, 0, 0)),
            whole(upper), whole(y), whole(z), whole(image), whole(back),
            pl.BlockSpec((tile, cols, width, width), lambda i: (i, 0, 0, 0)),
        ],
        out_specs=[pl.BlockSpec((tile, cols, width, width), lambda i: (i, 0, 0, 0))]
        + [whole(x) for x in outs[1:]],
        scratch_shapes=[
            pltpu.VMEM((2 * width, cols * width), BF16),
            pltpu.VMEM((2 * width, cols * width), BF16),
        ],
        compiler_params=pltpu.CompilerParams(vmem_limit_bytes=24 * 1024 * 1024),
    )(flags, fcol, upper, y, z, image, back, blocks)
    return (
        factored[:, None, :, None],
        direct[:, None],
        adjoint[:, None],
        image[:, None],
        back[:, None],
    )


def solution(mesh):
    placed = (
        P(None, "row", None, "col", None, None),
        P(None, "row", None, "col"),
        P(),
        P(None, "row", None, None),
        P(None, "row", None, None),
    )
    return jax.shard_map(
        shards,
        mesh=mesh,
        in_specs=placed,
        out_specs=(
            P(None, "row", None, "col", None, None),
            P(None, "row", None, None),
            P(None, "row", None, None),
            P(None, "row", "col", None),
            P(None, "col", "row", None),
        ),
        check_vma=False,
    )
```

time: 314 us -> 179 us (0.57)
  Pallas kernels: 0 us -> 172 us
  waiting for transfers between devices: 171 us -> 0 us
  blocking collectives: 51.1 us -> 0 us
  matrix products: 42.5 us -> 0 us
  other arithmetic: 16.2 us -> 0 us
  between operations: 14.3 us -> 0.64 us
  local copies, waits for them, and re-layouts: 18.6 us -> 6.85 us
    pallas_call x0 -> x2, Pallas kernels: none -> 172 us  [the longest x1 164 us: shards(): pl.pallas_call(functools.partial(comm_kernel, n_row, n_col), out_shape=(s...]
    psum x4 -> x0, waiting for transfers between devices: 146 us -> none  [from_root(): return lax.psum(jnp.where(mine, x, jnp.zeros_like(x)), axis)]
    dot_general x10 -> x0, matrix products: 42.5 us -> none  [the longest x2 20.5 us: apply_panel(): change = jnp.einsum('iab,jbc->ijac', lower, upper, precision=highest)]
    psum x2 -> x0, blocking collectives: 34.9 us -> none  [from_root(): return lax.psum(jnp.where(mine, x, jnp.zeros_like(x)), axis)]
    reduce_scatter x2 -> x0, waiting for transfers between devices: 24.6 us -> none  [the longest x1 24.6 us: shards(): lax.psum_scatter(image_terms, 'col', scatter_dimension=1, tiled=True)]
    all_gather x1 -> x0, blocking collectives: 16.2 us -> none  [shards(): gathered = lax.all_gather(solution[:, None], 'row', axis=1, tiled=True)]
    unnamed x22 -> x8, local copies, waits for them, and re-layouts: 17.2 us -> 6.09 us
    mul x1 -> x0, other arithmetic: 7.39 us -> none  [shards(): trace * fill[:, :, :, :, None, None].astype(jnp.float32)]
  transfers between devices with their start and end apart: 6 -> 0, of which waited for: 5 -> 0; matrix products, arithmetic and copies ran while one was open for 11% -> 0% of each run, Pallas kernels for 0% -> 0%
where the time goes in v1:
time: 179 us
  Pallas kernels  172 us (96%)
  local copies, waits for them, and re-layouts  6.85 us (4%)
    pallas_call x1, Pallas kernels, shards(): pl.pallas_call(functools.partial(comm_kernel, n_row, n_col), out_shape=(s...  164 us
    pallas_call x1, Pallas kernels, shards(): pl.pallas_call(functools.partial(update_kernel, n_row, tile), out_shape=o...  8.15 us
    unnamed x8, local copies, waits for them, and re-layouts  6.09 us

profile of v1, /device:TPU:0, one launch (start us, length us, event | category | flops | bytes accessed | tf_op | source)
XLA Modules:
  0.0 179.2 jit_solution(14456126210975912701)
XLA Ops:
  0.6 0.8 copy.11.fill
  1.4 0.0 copy-start
  1.4 3.4 %copy-done = f32[16,1,8,1,128,128]{5,4,3,2,1,0:T(8,128)S(1)} copy-done((f32[16,1,8,1,128,128]{5,4,3,2,1,0:T(8,128)S(1)}, f32[16,1,8,1,128,128]{5,4,3,2,1,0:T(8,128)}, u32[]{:S(2)}) %copy-start) | copy-done | bytes 8388632
  4.8 0.0 copy-start.1
  4.8 0.9 copy-done.1
  5.7 0.0 copy-start.2
  5.7 0.9 copy-done.2
  6.6 0.0 copy-start.3
  6.6 0.9 copy-done.3
  7.5 163.5 %shard_map.92 = (f32[2,16,128,128]{3,2,1,0:T(8,128)S(1)}, f32[2,8,128,128]{3,2,1,0:T(8,128)S(1)}, f32[16,16,128]{2,1,0:T(8,128)S(1)}, f32[16,16,128]{2,1,0:T(8,1...) custom-call(s32[16,8]{1,0:T(8,128)S(1)} %copy.11.fill, f32[2,128,128]{2,1,0:T(8,128)S(1)} %copy-done.1, ...), custom_call_target="tpu_custom_call" | custom-call | tf_op jit(solution)/shard_map/pallas_call | solution.py:503
  171.0 8.1 %shard_map.93 = (f32[16,8,128,128]{3,2,1,0:T(8,128)}, f32[16,16,128]{2,1,0:T(8,128)}, f32[16,16,128]{2,1,0:T(8,128)}, f32[16,2,128]{2,1,0:T(2,128)}, f32[8,4,128]{2,1,0:T(4,128)}) custom-call(s32[16,8]{1,0:T(8,128)S(1)} %copy.11.fill, f32[2,16,128,128]{3,2,1,0:T(8,128)S(1)} %get-tuple-element.16.fcol, f32[2,8,128,128]{3,2,1,0:T(8,128)S(1)} %get-tuple-element.17.upper, ...), custom_call_target="tpu_custom_call" | custom-call | tf_op jit(solution)/shard_map/pallas_call | solution.py:552
Async XLA Ops:
  1.4 3.4 %copy-start = (f32[16,1,8,1,128,128]{5,4,3,2,1,0:T(8,128)S(1)}, f32[16,1,8,1,128,128]{5,4,3,2,1,0:T(8,128)}, u32[]{:S(2)}) copy-start(f32[16,1,8,1,128,128]{5,4,3,2,1,0:T(8,128)} %param.5) | copy-start | bytes 25165828
  4.8 0.9 copy-start.1
  5.7 0.9 copy-start.2
  6.6 0.9 copy-start.3

commit v2 on v1

--- a/solution.py
+++ b/solution.py
@@ -42,13 +42,13 @@
 def comm_kernel(
     n_row, n_col, fill, piv, direct_rhs, adjoint_rhs, trace,
     fcol, upper, y_out, z_out, image, back,
-    colbuf, rowbuf, mbuf, small, wloc, wrecv, ysel, ypair, zpair,
+    colbuf, rowbuf, small, wloc, wrecv, ysel, ypair, zpair,
     img_p, img_t, img_r, back_p, back_t, back_r,
-    load_sem, m_sem, sm_send, sm_recv, ring_send, ring_recv, sib_send, sib_recv,
+    sm_send, sm_recv, ring_send, ring_recv, sib_send, sib_recv,
     row_up, row_down, row_recv, w_send, w_recv, y_send, y_recv,
     is_send, is_recv, bs_send, bs_recv,
 ):
-    rows, cols = mbuf.shape[0], mbuf.shape[1]
+    rows, cols = trace.shape[0], trace.shape[1]
     modes = y_out.shape[1]
     width = y_out.shape[2]
     img_modes, back_modes = modes // n_col, modes // n_row
@@ -76,20 +76,6 @@
             device_id=(row, col), device_id_type=pl.DeviceIdType.MESH,
         )
 
-    col_load = pltpu.make_async_copy(trace.at[:, 0], colbuf.at[core, pl.ds(0, rows)], load_sem.at[0])
-    row_load = pltpu.make_async_copy(trace.at[0], rowbuf.at[lax.rem(p, 2)], load_sem.at[1])
-
-    @pl.when(q < 2)
-    def _():
-        col_load.start()
-
-    @pl.when(p < 2)
-    def _():
-        row_load.start()
-
-    m_load = pltpu.make_async_copy(trace, mbuf, m_sem)
-    m_load.start()
-
     barrier = pltpu.get_barrier_semaphore()
     for d in range(1, n_col):
         pl.semaphore_signal(barrier, inc=1, device_id=(p, (q + d) % n_col), device_id_type=pl.DeviceIdType.MESH)
@@ -98,21 +84,18 @@
 
     @pl.when(q < 2)
     def _():
-        col_load.wait()
-
         def mask(a, _):
-            colbuf[core, a] = colbuf[core, a] * fill[a, 0].astype(F32)
+            colbuf[core, a] = trace[a, 0] * fill[a, 0].astype(F32)
             return 0
 
         lax.fori_loop(0, rows, mask, 0)
 
     @pl.when(p < 2)
     def _():
-        row_load.wait()
         slot = lax.rem(p, 2)
 
         def mask(c, _):
-            rowbuf[slot, c] = rowbuf[slot, c] * fill[0, c].astype(F32)
+            rowbuf[slot, c] = trace[0, c] * fill[0, c].astype(F32)
             return 0
 
         lax.fori_loop(0, cols, mask, 0)
@@ -202,33 +185,63 @@
                     def _():
                         row_copy(k, c, False).start()
 
-    def ring_pair(s, _):
-        ring_step(s, True)
-        ring_step(half + s, False)
+    def corner(dest, send, recv):
+        return to(rowbuf.at[1 - core, 0], colbuf.at[core, rows], send.at[rows], recv.at[rows], p, dest)
+
+    def back_row(a, first):
+        za = stack(adjoint_rhs[a])
+        for c in range(first, cols):
+            mh, ml = split(trace[a, c] * fill[a, c].astype(F32))
+            back_p[c] += thin(za, mh, ml, NN)
+
+    back_p[...] = jnp.zeros_like(back_p)
+    lag = 2
+    row_lag = 3
+    base = row_lag * jnp.maximum(p, 1)
+    ticks = max(half + lag * (chips - 1), row_lag * max(n_row - 1, 1) + lag * (chips - 1) + 2, rows)
+    last = n_row - 1
+
+    def row_tick(k):
+        d = k - base
+
+        @pl.when((d >= 0) & (d < 2 * cols) & ((d == 0) | (p != last)))
+        def _():
+            @pl.when(lax.rem(d, 2) == 0)
+            def _():
+                row_step(lax.div(d, 2))
+
+    def tick(k, _):
+        sa = k - lag * pos
+
+        @pl.when((sa >= 0) & (sa < half))
+        def _():
+            ring_step(sa, True)
+
+        sb = k - lag * (chips - pos)
+
+        @pl.when((sb >= 0) & (sb < half))
+        def _():
+            ring_step(half + sb, False)
+
+        row_tick(k)
+
+        @pl.when((pos == 0) & (k == base))
+        def _():
+            corner(after, ring_send, ring_recv).start()
+            corner(sibling, sib_send, sib_recv).start()
+            colbuf[core, rows] = rowbuf[1 - core, 0]
+
+        @pl.when(k == base + lag * pos + 1)
+        def _():
+            ring_step(rows, True)
+
+        @pl.when((k >= 1) & (k < rows))
+        def _():
+            back_row(k, 1)
+
         return 0
 
-    lax.fori_loop(0, half // 2, ring_pair, 0)
-    row_step(0)
-
-    @pl.when(pos == 0)
-    def _():
-        colbuf[core, rows] = rowbuf[1 - core, 0]
-        lax.fori_loop(half // 2, half - 2, ring_pair, 0)
-
-    @pl.when(pos != 0)
-    def _():
-        lax.fori_loop(half // 2, half - 2, ring_pair, 0)
-
-    row_step(1)
-
-    @pl.when(pos == 0)
-    def _():
-        ring(rows, after).start()
-        sib(rows, core).start()
-
-    lax.fori_loop(half - 2, half, ring_pair, 0)
-    row_step(2)
-    ring_step(rows, True)
+    lax.fori_loop(0, ticks, tick, 0)
 
     def sib_wait(block, _):
         sib(block, 1 - core).wait_recv()
@@ -240,7 +253,6 @@
         def _(k=k):
             for kind in range(2):
                 to(small.at[k, kind], small.at[k, kind], sm_send.at[kind, 0], sm_recv.at[k, kind], p, sibling).wait_recv()
-    row_step(3)
 
     p0h, p0l = split(piv[0])
     p1h, p1l = split(piv[1])
@@ -272,8 +284,8 @@
     quarter = rows // 4
     for g in range(4):
         lax.fori_loop(g * quarter, (g + 1) * quarter, form, 0)
-        if g < 3:
-            row_step(4 + g)
+        row_tick(ticks + 2 * g)
+        row_tick(ticks + 2 * g + 1)
 
     owner = q % n_row
     step = n_col // n_row
@@ -296,8 +308,19 @@
         for d in range(1, n_row):
             y_copy(d).start()
 
-    for c in range(7, cols):
-        row_step(c)
+    def late(k, _):
+        row_tick(k)
+        return 0
+
+    lax.fori_loop(ticks + 8, max(ticks + 8, row_lag * max(n_row - 1, 1) + 2 * cols), late, 0)
+
+    @pl.when(p == last)
+    def _():
+        def arrive(c, _):
+            row_step(c)
+            return 0
+
+        lax.fori_loop(1, cols, arrive, 0)
 
     def form_upper(c, _):
         u0 = rowbuf[0, c]
@@ -323,8 +346,6 @@
     @pl.when(p != owner)
     def _():
         to(ysel, ysel, y_send.at[0], y_recv, p, sibling).wait_recv()
-
-    m_load.wait()
 
     wz0 = stack(wloc[0] + jnp.where(p == 1, 1.0, 0.0) * z1l)
     wz1 = stack(wloc[1])
@@ -338,7 +359,7 @@
         u1h, u1l = split(upper[1, c] * inner)
         v0 = v0 + thin(yc, u0h, u0l, NT)
         v1 = v1 + thin(yc, u1h, u1l, NT)
-        back_p[c] = -(thin(wz0, u0h, u0l, NN) + thin(wz1, u1h, u1l, NN))
+        back_p[c] -= (thin(wz0, u0h, u0l, NN) + thin(wz1, u1h, u1l, NN))
     v0 = stack(v0)
     v1 = stack(v1)
 
@@ -349,16 +370,21 @@
         l1h, l1l = split(fcol[1, a] * jnp.where(index > 1, 1.0, 0.0))
         acc = -(thin(v0, l0h, l0l, NT) + thin(v1, l1h, l1l, NT))
         for c in range(cols):
-            m = mbuf[a, c] * fill[a, c].astype(F32)
+            m = trace[a, c] * fill[a, c].astype(F32)
             if c == 0:
                 m = jnp.where(q == 0, fcol[0, a], jnp.where(q == 1, fcol[1, a], m))
             mh, ml = split(m)
             acc = acc + thin(ypair[c], mh, ml, NT)
-            back_p[c] += thin(za, mh, ml, NN)
+            if c == 0:
+                back_p[c] += thin(za, mh, ml, NN)
         img_p[a] = acc
         return 0
 
     lax.fori_loop(0, rows, products, 0)
+    first = stack(z_out[0])
+    for c in range(1, cols):
+        mh, ml = split(trace[0, c] * fill[0, c].astype(F32))
+        back_p[c] += thin(first, mh, ml, NN)
     for m in range(modes):
         img_t[m] = img_p[:, m, :] * scale
         back_t[m] = back_p[:, m, :] * scale
@@ -510,12 +536,11 @@
             shape((mi, rows, width), F32),
             shape((mb, cols, width), F32),
         ),
-        in_specs=[smem, vmem, vmem, vmem, pl.BlockSpec(memory_space=pl.ANY)],
+        in_specs=[smem, vmem, vmem, vmem, vmem],
         out_specs=[vmem] * 6,
         scratch_shapes=[
             pltpu.VMEM((2, rows + 1, width, width), F32),
             pltpu.VMEM((2, cols, width, width), F32),
-            pltpu.VMEM((rows, cols, width, width), F32),
             pltpu.VMEM((2, 2, modes, width), F32),
             pltpu.VMEM((2, modes, width), F32),
             pltpu.VMEM((n_row, 2, modes, width), F32),
@@ -528,7 +553,6 @@
             pltpu.VMEM((cols, modes, width), F32),
             pltpu.VMEM((modes, cols, width), F32),
             pltpu.VMEM((n_row, mb, cols, width), F32),
-            dma((2,)), dma,
             dma((2, n_row)), dma((2, 2)),
             dma((rows + 1,)), dma((rows + 1,)), dma((rows + 1,)), dma((rows + 1,)),
             dma((2, cols)), dma((2, cols)), dma((2, cols)),

time: 179 us -> 82.9 us (0.46)
  Pallas kernels: 172 us -> 75.2 us
    pallas_call x1, Pallas kernels: 164 us -> 67 us  [shards(): pl.pallas_call(functools.partial(comm_kernel, n_row, n_col), out_shape=(s...]
where the time goes in v2:
time: 82.9 us; the launch traced here: 82.7 us
  Pallas kernels  75.2 us (91%)
  local copies, waits for them, and re-layouts  6.85 us (8%)
    pallas_call x1, Pallas kernels, shards(): pl.pallas_call(functools.partial(comm_kernel, n_row, n_col), out_shape=(s...  67 us
    pallas_call x1, Pallas kernels, shards(): pl.pallas_call(functools.partial(update_kernel, n_row, tile), out_shape=o...  8.14 us
    unnamed x8, local copies, waits for them, and re-layouts  6.09 us

profile of v2, /device:TPU:0, one launch (start us, length us, event | category | flops | bytes accessed | tf_op | source)
XLA Modules:
  0.0 82.7 jit_solution(5333355944281671727)
XLA Ops:
  0.6 0.8 copy.11.fill
  1.4 0.0 copy-start
  1.4 3.4 %copy-done = f32[16,1,8,1,128,128]{5,4,3,2,1,0:T(8,128)S(1)} copy-done((f32[16,1,8,1,128,128]{5,4,3,2,1,0:T(8,128)S(1)}, f32[16,1,8,1,128,128]{5,4,3,2,1,0:T(8,128)}, u32[]{:S(2)}) %copy-start) | copy-done | bytes 8388632
  4.8 0.0 copy-start.1
  4.8 0.9 %copy-done.1 = f32[2,128,128]{2,1,0:T(8,128)S(1)} copy-done((f32[2,128,128]{2,1,0:T(8,128)S(1)}, f32[2,128,128]{2,1,0:T(8,128)}, u32[]{:S(2)}) %copy-start.1) | copy-done | bytes 131096
  5.7 0.0 copy-start.2
  5.7 0.9 %copy-done.2 = f32[16,1,16,128]{3,2,1,0:T(8,128)S(1)} copy-done((f32[16,1,16,128]{3,2,1,0:T(8,128)S(1)}, f32[16,1,16,128]{3,2,1,0:T(8,128)}, u32[]{:S(2)}) %copy-start.2) | copy-done | bytes 131096
  6.6 0.0 copy-start.3
  6.6 0.9 %copy-done.3 = f32[16,1,16,128]{3,2,1,0:T(8,128)S(1)} copy-done((f32[16,1,16,128]{3,2,1,0:T(8,128)S(1)}, f32[16,1,16,128]{3,2,1,0:T(8,128)}, u32[]{:S(2)}) %copy-start.3) | copy-done | bytes 131096
  7.5 67.0 %shard_map.92 = (f32[2,16,128,128]{3,2,1,0:T(8,128)S(1)}, f32[2,8,128,128]{3,2,1,0:T(8,128)S(1)}, f32[16,16,128]{2,1,0:T(8,128)S(1)}, f32[16,16,128]{2,1,0:T(8,1...) custom-call(s32[16,8]{1,0:T(8,128)S(1)} %copy.11.fill, f32[2,128,128]{2,1,0:T(8,128)S(1)} %copy-done.1, ...), custom_call_target="tpu_custom_call" | custom-call | tf_op jit(solution)/shard_map/pallas_call | solution.py:529
  74.5 8.1 %shard_map.93 = (f32[16,8,128,128]{3,2,1,0:T(8,128)}, f32[16,16,128]{2,1,0:T(8,128)}, f32[16,16,128]{2,1,0:T(8,128)}, f32[16,2,128]{2,1,0:T(2,128)}, f32[8,4,128]{2,1,0:T(4,128)}) custom-call(s32[16,8]{1,0:T(8,128)S(1)} %copy.11.fill, f32[2,16,128,128]{3,2,1,0:T(8,128)S(1)} %get-tuple-element.16.fcol, f32[2,8,128,128]{3,2,1,0:T(8,128)S(1)} %get-tuple-element.17.upper, ...), custom_call_target="tpu_custom_call" | custom-call | tf_op jit(solution)/shard_map/pallas_call | solution.py:576
Async XLA Ops:
  1.4 3.4 %copy-start = (f32[16,1,8,1,128,128]{5,4,3,2,1,0:T(8,128)S(1)}, f32[16,1,8,1,128,128]{5,4,3,2,1,0:T(8,128)}, u32[]{:S(2)}) copy-start(f32[16,1,8,1,128,128]{5,4,3,2,1,0:T(8,128)} %param.5) | copy-start | bytes 25165828
  4.8 0.9 %copy-start.1 = (f32[2,128,128]{2,1,0:T(8,128)S(1)}, f32[2,128,128]{2,1,0:T(8,128)}, u32[]{:S(2)}) copy-start(f32[2,128,128]{2,1,0:T(8,128)} %piv.1) | copy-start | bytes 393220
  5.7 0.9 %copy-start.2 = (f32[16,1,16,128]{3,2,1,0:T(8,128)S(1)}, f32[16,1,16,128]{3,2,1,0:T(8,128)}, u32[]{:S(2)}) copy-start(f32[16,1,16,128]{3,2,1,0:T(8,128)} %param.8) | copy-start | bytes 393220
  6.6 0.9 %copy-start.3 = (f32[16,1,16,128]{3,2,1,0:T(8,128)S(1)}, f32[16,1,16,128]{3,2,1,0:T(8,128)}, u32[]{:S(2)}) copy-start(f32[16,1,16,128]{3,2,1,0:T(8,128)} %param.9) | copy-start | bytes 393220

commit v3 on v2

--- a/solution.py
+++ b/solution.py
@@ -40,7 +40,7 @@
 
 
 def comm_kernel(
-    n_row, n_col, fill, piv, direct_rhs, adjoint_rhs, trace,
+    n_row, n_col, fill, packed, trace,
     fcol, upper, y_out, z_out, image, back,
     colbuf, rowbuf, small, wloc, wrecv, ysel, ypair, zpair,
     img_p, img_t, img_r, back_p, back_t, back_r,
@@ -49,6 +49,7 @@
     is_send, is_recv, bs_send, bs_recv,
 ):
     rows, cols = trace.shape[0], trace.shape[1]
+    direct_rhs, adjoint_rhs = packed.at[0], packed.at[1]
     modes = y_out.shape[1]
     width = y_out.shape[2]
     img_modes, back_modes = modes // n_col, modes // n_row
@@ -196,7 +197,8 @@
 
     back_p[...] = jnp.zeros_like(back_p)
     lag = 2
-    row_lag = 3
+    row_lag = 4
+    stride = 2
     base = row_lag * jnp.maximum(p, 1)
     ticks = max(half + lag * (chips - 1), row_lag * max(n_row - 1, 1) + lag * (chips - 1) + 2, rows)
     last = n_row - 1
@@ -204,11 +206,11 @@
     def row_tick(k):
         d = k - base
 
-        @pl.when((d >= 0) & (d < 2 * cols) & ((d == 0) | (p != last)))
-        def _():
-            @pl.when(lax.rem(d, 2) == 0)
+        @pl.when((d >= 0) & (d < stride * cols) & ((d == 0) | (p != last)))
+        def _():
+            @pl.when(lax.rem(d, stride) == 0)
             def _():
-                row_step(lax.div(d, 2))
+                row_step(lax.div(d, stride))
 
     def tick(k, _):
         sa = k - lag * pos
@@ -254,8 +256,9 @@
             for kind in range(2):
                 to(small.at[k, kind], small.at[k, kind], sm_send.at[kind, 0], sm_recv.at[k, kind], p, sibling).wait_recv()
 
-    p0h, p0l = split(piv[0])
-    p1h, p1l = split(piv[1])
+    per = width // modes
+    p0h, p0l = split(packed[2, 0:per].reshape(width, width))
+    p1h, p1l = split(packed[2, per:2 * per].reshape(width, width))
     u01h, u01l = split(colbuf[1, rows])
     c10h, c10l = split(colbuf[0, rows])
     l10 = mul(c10h, p0h, NN) + mul(c10h, p0l, NN) + mul(c10l, p0h, NN)
@@ -312,7 +315,7 @@
         row_tick(k)
         return 0
 
-    lax.fori_loop(ticks + 8, max(ticks + 8, row_lag * max(n_row - 1, 1) + 2 * cols), late, 0)
+    lax.fori_loop(ticks + 8, max(ticks + 8, row_lag * max(n_row - 1, 1) + stride * cols), late, 0)
 
     @pl.when(p == last)
     def _():
@@ -521,6 +524,9 @@
     blocks = trace.reshape(rows, cols, width, width)
     flags = fill.reshape(rows, cols)
     direct_rhs, adjoint_rhs = direct_rhs[:, 0], adjoint_rhs[:, 0]
+    tiles = pivots.reshape(-1, modes, width)
+    tiles = jnp.pad(tiles, ((0, max(0, rows - tiles.shape[0])), (0, 0), (0, 0)))
+    packed = jnp.stack([direct_rhs, adjoint_rhs, tiles])
     mi, mb = modes // n_col, modes // n_row
     vmem = pl.BlockSpec(memory_space=pltpu.VMEM)
     smem = pl.BlockSpec(memory_space=pltpu.SMEM)
@@ -536,7 +542,7 @@
             shape((mi, rows, width), F32),
             shape((mb, cols, width), F32),
         ),
-        in_specs=[smem, vmem, vmem, vmem, vmem],
+        in_specs=[smem, vmem, vmem],
         out_specs=[vmem] * 6,
         scratch_shapes=[
             pltpu.VMEM((2, rows + 1, width, width), F32),
@@ -562,9 +568,9 @@
         compiler_params=pltpu.CompilerParams(
             collective_id=0, has_side_effects=True, vmem_limit_bytes=40 * 1024 * 1024
         ),
-    )(flags, pivots, direct_rhs, adjoint_rhs, blocks)
-
-    tile = 2
+    )(flags, packed, blocks)
+
+    tile = 4
     whole = lambda x: pl.BlockSpec(x.shape, lambda i: (0,) * x.ndim)
     outs = (
         shape(blocks.shape, F32),
@@ -589,7 +595,7 @@
             pltpu.VMEM((2 * width, cols * width), BF16),
             pltpu.VMEM((2 * width, cols * width), BF16),
         ],
-        compiler_params=pltpu.CompilerParams(vmem_limit_bytes=24 * 1024 * 1024),
+        compiler_params=pltpu.CompilerParams(vmem_limit_bytes=32 * 1024 * 1024),
     )(flags, fcol, upper, y, z, image, back, blocks)
     return (
         factored[:, None, :, None],

time: 82.9 us -> 78.9 us (0.952)
  local copies, waits for them, and re-layouts: 6.85 us -> 4.14 us
  Pallas kernels: 75.2 us -> 72.8 us
  other arithmetic: 0 us -> 1.06 us
    unnamed x8 -> x4, local copies, waits for them, and re-layouts: 6.09 us -> 3.38 us
    pallas_call x1, Pallas kernels: 67 us -> 65.8 us  [shards(): pl.pallas_call(functools.partial(comm_kernel, n_row, n_col), out_shape=(s...]
    pallas_call x1, Pallas kernels: 8.14 us -> 6.97 us  [shards(): pl.pallas_call(functools.partial(update_kernel, n_row, tile), out_shape=o...]
    another operation x0 -> x1, other arithmetic: none -> 1.06 us  [shards(): packed = jnp.stack([direct_rhs, adjoint_rhs, tiles])]
where the time goes in v3:
time: 78.9 us; the launch traced here: 78.7 us
  Pallas kernels  72.8 us (92%)
  local copies, waits for them, and re-layouts  4.14 us (5%)
  other arithmetic  1.06 us (1%)
    pallas_call x1, Pallas kernels, shards(): pl.pallas_call(functools.partial(comm_kernel, n_row, n_col), out_shape=(s...  65.8 us
    pallas_call x1, Pallas kernels, shards(): pl.pallas_call(functools.partial(update_kernel, n_row, tile), out_shape=o...  6.97 us
    unnamed x4, local copies, waits for them, and re-layouts  3.38 us

profile of v3, /device:TPU:0, one launch (start us, length us, event | category | flops | bytes accessed | tf_op | source)
XLA Modules:
  0.0 78.7 jit_solution(17253263399104007762)
XLA Ops:
  0.6 0.8 copy.11.fill
  1.4 1.1 %pad_maximum_fusion.packed = f32[3,16,16,128]{3,2,1,0:T(8,128)S(1)} fusion(f32[1,16,16,128]{3,2,1,0:T(8,128)} %bitcast.22, f32[1,16,16,128]{3,2,1,0:T(8,128)} %bitcast.23, f32[1,16,16,128]{3,2,1,0:T(8,128)} %bitcast.24), kind=kLoop, calls=%fused_computation | loop fusion | flops 196608 | bytes 786432 | tf_op jit(solution)/shard_map/stack | solution.py:529
  2.4 0.0 copy-start
  2.5 3.4 %copy-done = f32[16,1,8,1,128,128]{5,4,3,2,1,0:T(8,128)S(1)} copy-done((f32[16,1,8,1,128,128]{5,4,3,2,1,0:T(8,128)S(1)}, f32[16,1,8,1,128,128]{5,4,3,2,1,0:T(8,128)}, u32[]{:S(2)}) %copy-start) | copy-done | bytes 8388632
  5.8 0.0 copy-start.1
  5.8 65.8 %shard_map.92 = (f32[2,16,128,128]{3,2,1,0:T(8,128)S(1)}, f32[2,8,128,128]{3,2,1,0:T(8,128)S(1)}, f32[16,16,128]{2,1,0:T(8,128)S(1)}, f32[16,16,128]{2,1,0:T(8,1...) custom-call(s32[16,8]{1,0:T(8,128)S(1)} %copy.11.fill, f32[3,16,16,128]{3,2,1,0:T(8,128)S(1)} %pad_maximum_fusion.packed, ...), custom_call_target="tpu_custom_call" | custom-call | tf_op jit(solution)/shard_map/pallas_call | solution.py:535
  71.7 0.0 copy-done.1
  71.7 7.0 %shard_map.93 = (f32[16,8,128,128]{3,2,1,0:T(8,128)}, f32[16,16,128]{2,1,0:T(8,128)}, f32[16,16,128]{2,1,0:T(8,128)}, f32[16,2,128]{2,1,0:T(2,128)}, f32[8,4,128]{2,1,0:T(4,128)}) custom-call(s32[16,8]{1,0:T(8,128)S(1)} %copy.11.fill, f32[2,16,128,128]{3,2,1,0:T(8,128)S(1)} %get-tuple-element.16.fcol, f32[2,8,128,128]{3,2,1,0:T(8,128)S(1)} %get-tuple-element.17.upper, ...), custom_call_target="tpu_custom_call" | custom-call | tf_op jit(solution)/shard_map/pallas_call | solution.py:582
Async XLA Ops:
  2.4 3.4 %copy-start = (f32[16,1,8,1,128,128]{5,4,3,2,1,0:T(8,128)S(1)}, f32[16,1,8,1,128,128]{5,4,3,2,1,0:T(8,128)}, u32[]{:S(2)}) copy-start(f32[16,1,8,1,128,128]{5,4,3,2,1,0:T(8,128)} %param.5) | copy-start | bytes 25165828
  5.8 65.8 %copy-start.1 = (f32[16,1,8,1,128,128]{5,4,3,2,1,0:T(8,128)S(1)}, f32[16,1,8,1,128,128]{5,4,3,2,1,0:T(8,128)}, u32[]{:S(2)}) copy-start(f32[16,1,8,1,128,128]{5,4,3,2,1,0:T(8,128)} %param.5) | copy-start | bytes 25165828
